TPU v7x, 128 devices: a whole 4x4x4 slice. The times are simulated.
128 devices in a mesh: row: 16 (over z_hi, y, core), col: 8 (over z_lo, x).
Axes of the slice: x: 4, y: 4, z: 4 (z_hi: 2, z_lo: 2; z = z_hi * 2 + z_lo), core: 2. Of those that a mesh axis runs over, the one named last changes fastest.
Arguments:
- grad_out: bfloat16 [262144, 256], P(('row', 'col')), may hold values from -6 to 6
- preact: bfloat16 [262144, 256], P(('row', 'col')), may hold values from -6 to 6
- features: bfloat16 [262144, 256], P(('col', 'row')), may hold values from -6 to 6
- weight: bfloat16 [256, 256], replicated, may hold values from -0.375 to 0.375
- tiles: bfloat16 [16, 8, 320, 128, 128], P('row', 'col'), may hold values from -0.099609375 to 0.099609375
- tile_rows: int32 [16, 8, 320], P('row', 'col'), may hold values from 0 to 127
- tile_cols: int32 [16, 8, 320], P('row', 'col'), may hold values from 0 to 255
- live_counts: int32 [16, 8], P('row', 'col'), may hold values from 80 to 320, as said below
Outputs:
- grad_features: bfloat16 [262144, 256], P(('col', 'row'))
- grad_weight: float32 [256, 256], replicated
Inputs may be any that keep to these rules, and one draw needn't show every extreme that they name: `live_counts`: some block holds exactly 320 live tiles in every draw.
All inputs are finite; a program needn't handle non-finite values.
Results may differ from a plain program's by a relative error of at most 0.02.
Values may be sent and summed in bfloat16 or wider, within the bound.
A program may use at most 192 MiB of HBM per device.

v0:
```python
import math
import jax
import jax.numpy as jnp
from jax import lax
from jax.sharding import PartitionSpec as P


def body(grad_out, preact, features, weight, tiles, tile_rows, tile_cols, live_counts):
    width = grad_out.shape[1]
    masked = jnp.where(preact > 0, grad_out, jnp.zeros_like(grad_out))
    block = lax.all_gather(masked, "col", axis=0, tiled=True)
    row_count = block.shape[0] // 128
    row_flat = block.reshape(row_count, 128 * width)
    slots = tiles.shape[2]
    tile_stack = tiles.reshape(slots, 128, 128)
    row_index = tile_rows.reshape(slots)
    col_index = tile_cols.reshape(slots)
    count = live_counts.reshape(())
    col_tiles = lax.axis_size("row") * grad_out.shape[0] // 128
    group = math.gcd(slots, 32)
    offsets = jnp.arange(group, dtype=jnp.int32)
    row_ids = jnp.arange(row_count, dtype=jnp.int32)
    col_ids = jnp.arange(col_tiles, dtype=jnp.int32)

    def add_group(step, accum):
        start = step * group
        tile_blk = lax.dynamic_slice_in_dim(tile_stack, start, group, 0)
        rows_now = lax.dynamic_slice_in_dim(row_index, start, group, 0)
        cols_now = lax.dynamic_slice_in_dim(col_index, start, group, 0) - 0
        pick = (rows_now[:, None] == row_ids[None, :]).astype(jnp.bfloat16)
        gathered = jnp.dot(pick, row_flat, preferred_element_type=jnp.float32).astype(jnp.bfloat16)
        gathered = gathered.reshape(group, 128, width)
        prod = jnp.einsum("kab,kaf->kbf", tile_blk, gathered, preferred_element_type=jnp.float32)
        upper = prod.astype(jnp.bfloat16)
        lower = (prod - upper.astype(jnp.float32)).astype(jnp.bfloat16)
        keep = start + offsets < count
        place = ((cols_now[None, :] == col_ids[:, None]) & keep[None, :]).astype(jnp.bfloat16)
        both_place = jnp.concatenate([place, place], axis=1)
        both_vals = jnp.concatenate([upper, lower], axis=0).reshape(2 * group, 128 * width)
        return accum + jnp.dot(both_place, both_vals, preferred_element_type=jnp.float32)

    accum = jnp.zeros((col_tiles, 128 * width), jnp.float32)
    accum = lax.fori_loop(0, slots // group, add_group, accum)
    partial_value = accum.reshape(col_tiles * 128, width)
    summed = lax.psum_scatter(
        partial_value.astype(jnp.bfloat16), "row", scatter_dimension=0, tiled=True
    )
    grad_features = lax.dot_general(
        summed, weight, (((1,), (1,)), ((), ())), preferred_element_type=jnp.float32
    ).astype(jnp.bfloat16)
    weight_term = lax.dot_general(
        features, summed, (((0,), (0,)), ((), ())), preferred_element_type=jnp.float32
    )
    grad_weight = lax.psum(weight_term, ("row", "col"))
    return (grad_features, grad_weight)


def solution(mesh):
    in_specs = (
        P(("row", "col"), None),
        P(("row", "col"), None),
        P(("col", "row"), None),
        P(),
        P("row", "col", None, None, None),
        P("row", "col", None),
        P("row", "col", None),
        P("row", "col"),
    )
    out_specs = (P(("col", "row"), None), P())
    return jax.shard_map(body, mesh=mesh, in_specs=in_specs, out_specs=out_specs, check_vma=False)
```

profile of v0, /device:TPU:1, one launch (start us, length us, event | category | flops | bytes accessed | tf_op | source)
XLA Modules:
  0.0 803.8 jit_solution(6973166508205975980)
XLA Ops:
  10.1 14.5 %copy.12 = bf16[1,1,320,128,128]{3,4,2,1,0:T(8,128)(2,1)} copy(bf16[1,1,320,128,128]{4,3,2,1,0:T(8,128)(2,1)} %param.14) | data formatting | bytes 20971520 | tf_op args[4]
  24.6 80.9 %all-gather.2.cloned.1.call-done = bf16[16384,256]{1,0:T(8,128)(2,1)} async-done(((bf16[2048,256]{1,0:T(8,128)(2,1)}), bf16[16384,256]{1,0:T(8,128)(2,1)}) %all-gather.2.cloned.1.call-update) | async-done | bytes 8388624 | tf_op jit(solution)/shard_map/all_gather | solution.py:11
  105.4 13.4 %reshape.49 = bf16[128,32768]{1,0:T(8,128)(2,1)} reshape(bf16[16384,256]{1,0:T(8,128)(2,1)} %all-gather.2.cloned.1.call-done) | data formatting | bytes 16777216 | tf_op jit(solution)/shard_map/reshape | solution.py:13
  118.9 342.9 %while.14 = (s32[]{:T(128)}, f32[256,32768]{1,0:T(8,128)}, s32[320]{0:T(512)S(1)}, s32[]{:T(128)}, bf16[320,128,128]{1,2,0:T(8,128)(2,1)}, /*index=5*/s32[320]{0...) while((s32[]{:T(128)}, f32[256,32768]{1,0:T(8,128)}, ...), condition=%wide.region_1.2_spmd.clone, body=%wide.region_0.1_spmd.clone.sunk | while | flops 1634766848 | bytes 110117888 | solution.py:43
  129.8 12.4 %convolution_add_fusion.2 = f32[256,32768]{1,0:T(8,128)} fusion(bf16[64,32768]{1,0:T(8,128)(2,1)S(1)} %bitcast.29, f32[256,32768]{1,0:T(8,128)} %get-tuple-element.281, pred[]{:T(512)S(6)} %compare.3, pred[256,32]{0,1:T(32,128)(4,1)S(1)} %fusion.34), kind=kOutput, calls=%fused_computation.3.clone.1 | convolution fusion | flops 1090535424 | bytes 71311360 | tf_op jit(solution)/shard_map/while/body/eval_jaxpr/dot_general | solution.py:40
  143.2 4.6 convolution_convert_fusion.3
  153.2 24.6 %convolution_add_fusion.2 = f32[256,32768]{1,0:T(8,128)} fusion(bf16[64,32768]{1,0:T(8,128)(2,1)S(1)} %bitcast.29, f32[256,32768]{1,0:T(8,128)} %get-tuple-element.281, pred[]{:T(512)S(6)} %compare.3, pred[256,32]{0,1:T(32,128)(4,1)S(1)} %fusion.34), kind=kOutput, calls=%fused_computation.3.clone.1 | convolution fusion | flops 1090535424 | bytes 71311360 | tf_op jit(solution)/shard_map/while/body/eval_jaxpr/dot_general | solution.py:40
  178.7 4.6 convolution_convert_fusion.3
  188.7 24.6 %convolution_add_fusion.2 = f32[256,32768]{1,0:T(8,128)} fusion(bf16[64,32768]{1,0:T(8,128)(2,1)S(1)} %bitcast.29, f32[256,32768]{1,0:T(8,128)} %get-tuple-element.281, pred[]{:T(512)S(6)} %compare.3, pred[256,32]{0,1:T(32,128)(4,1)S(1)} %fusion.34), kind=kOutput, calls=%fused_computation.3.clone.1 | convolution fusion | flops 1090535424 | bytes 71311360 | tf_op jit(solution)/shard_map/while/body/eval_jaxpr/dot_general | solution.py:40
  214.2 4.6 convolution_convert_fusion.3
  224.2 24.6 %convolution_add_fusion.2 = f32[256,32768]{1,0:T(8,128)} fusion(bf16[64,32768]{1,0:T(8,128)(2,1)S(1)} %bitcast.29, f32[256,32768]{1,0:T(8,128)} %get-tuple-element.281, pred[]{:T(512)S(6)} %compare.3, pred[256,32]{0,1:T(32,128)(4,1)S(1)} %fusion.34), kind=kOutput, calls=%fused_computation.3.clone.1 | convolution fusion | flops 1090535424 | bytes 71311360 | tf_op jit(solution)/shard_map/while/body/eval_jaxpr/dot_general | solution.py:40
  249.7 4.6 convolution_convert_fusion.3
  259.7 24.6 %convolution_add_fusion.2 = f32[256,32768]{1,0:T(8,128)} fusion(bf16[64,32768]{1,0:T(8,128)(2,1)S(1)} %bitcast.29, f32[256,32768]{1,0:T(8,128)} %get-tuple-element.281, pred[]{:T(512)S(6)} %compare.3, pred[256,32]{0,1:T(32,128)(4,1)S(1)} %fusion.34), kind=kOutput, calls=%fused_computation.3.clone.1 | convolution fusion | flops 1090535424 | bytes 71311360 | tf_op jit(solution)/shard_map/while/body/eval_jaxpr/dot_general | solution.py:40
  295.2 24.6 %convolution_add_fusion.2 = f32[256,32768]{1,0:T(8,128)} fusion(bf16[64,32768]{1,0:T(8,128)(2,1)S(1)} %bitcast.29, f32[256,32768]{1,0:T(8,128)} %get-tuple-element.281, pred[]{:T(512)S(6)} %compare.3, pred[256,32]{0,1:T(32,128)(4,1)S(1)} %fusion.34), kind=kOutput, calls=%fused_computation.3.clone.1 | convolution fusion | flops 1090535424 | bytes 71311360 | tf_op jit(solution)/shard_map/while/body/eval_jaxpr/dot_general | solution.py:40
  330.7 24.6 %convolution_add_fusion.2 = f32[256,32768]{1,0:T(8,128)} fusion(bf16[64,32768]{1,0:T(8,128)(2,1)S(1)} %bitcast.29, f32[256,32768]{1,0:T(8,128)} %get-tuple-element.281, pred[]{:T(512)S(6)} %compare.3, pred[256,32]{0,1:T(32,128)(4,1)S(1)} %fusion.34), kind=kOutput, calls=%fused_computation.3.clone.1 | convolution fusion | flops 1090535424 | bytes 71311360 | tf_op jit(solution)/shard_map/while/body/eval_jaxpr/dot_general | solution.py:40
  366.2 24.6 %convolution_add_fusion.2 = f32[256,32768]{1,0:T(8,128)} fusion(bf16[64,32768]{1,0:T(8,128)(2,1)S(1)} %bitcast.29, f32[256,32768]{1,0:T(8,128)} %get-tuple-element.281, pred[]{:T(512)S(6)} %compare.3, pred[256,32]{0,1:T(32,128)(4,1)S(1)} %fusion.34), kind=kOutput, calls=%fused_computation.3.clone.1 | convolution fusion | flops 1090535424 | bytes 71311360 | tf_op jit(solution)/shard_map/while/body/eval_jaxpr/dot_general | solution.py:40
  391.7 4.6 convolution_convert_fusion.3
  401.7 24.6 %convolution_add_fusion.2 = f32[256,32768]{1,0:T(8,128)} fusion(bf16[64,32768]{1,0:T(8,128)(2,1)S(1)} %bitcast.29, f32[256,32768]{1,0:T(8,128)} %get-tuple-element.281, pred[]{:T(512)S(6)} %compare.3, pred[256,32]{0,1:T(32,128)(4,1)S(1)} %fusion.34), kind=kOutput, calls=%fused_computation.3.clone.1 | convolution fusion | flops 1090535424 | bytes 71311360 | tf_op jit(solution)/shard_map/while/body/eval_jaxpr/dot_general | solution.py:40
  427.2 4.6 convolution_convert_fusion.3
  437.2 24.6 %convolution_add_fusion.2 = f32[256,32768]{1,0:T(8,128)} fusion(bf16[64,32768]{1,0:T(8,128)(2,1)S(1)} %bitcast.29, f32[256,32768]{1,0:T(8,128)} %get-tuple-element.281, pred[]{:T(512)S(6)} %compare.3, pred[256,32]{0,1:T(32,128)(4,1)S(1)} %fusion.34), kind=kOutput, calls=%fused_computation.3.clone.1 | convolution fusion | flops 1090535424 | bytes 71311360 | tf_op jit(solution)/shard_map/while/body/eval_jaxpr/dot_general | solution.py:40
  461.8 17.1 %convert_element_type.45 = bf16[256,32768]{1,0:T(8,128)(2,1)} convert(f32[256,32768]{1,0:T(8,128)} %get-tuple-element.171) | non-fusion elementwise | flops 8388608 | bytes 50331648 | tf_op jit(solution)/shard_map/convert_element_type | solution.py:46
  478.9 25.6 %convert_element_type.46 = bf16[32768,256]{1,0:T(8,128)(2,1)} reshape(bf16[256,32768]{1,0:T(8,128)(2,1)} %convert_element_type.45) | data formatting | bytes 33554432 | tf_op jit(solution)/shard_map/convert_element_type | solution.py:46
  504.6 145.1 %reduce-scatter.2.cloned.1.call-done = bf16[2048,256]{1,0:T(8,128)(2,1)} async-done(((bf16[32768,256]{1,0:T(8,128)(2,1)}), bf16[2048,256]{1,0:T(8,128)(2,1)}) %reduce-scatter.2.cloned.1.call-update) | async-done | bytes 1048592 | tf_op jit(solution)/shard_map/reduce_scatter | solution.py:45
  654.8 140.8 %all-reduce.2.cloned.1.call-done = f32[256,256]{0,1:T(8,128)} async-done(((f32[256,256]{0,1:T(8,128)}), f32[256,256]{0,1:T(8,128)}) %all-reduce.2.cloned.1.call-update) | async-done | bytes 262160 | tf_op jit(solution)/shard_map/psum | solution.py:54
  (105 shorter events, 90.7 us)
Async XLA Ops:
  7.2 642.5 %copy-start = (bf16[2048,256]{1,0:T(8,128)(2,1)S(1)}, bf16[2048,256]{1,0:T(8,128)(2,1)}, u32[]{:S(2)}) copy-start(bf16[2048,256]{1,0:T(8,128)(2,1)} %param.12) | copy-start | bytes 3145732
  7.2 2.9 copy-start.2
  7.2 2.9 copy-start.3
  7.2 98.2 %all-gather.2.cloned.1.call-start = ((), (), s32[]{:S(2)}) async-start(), calls=%async_computation.1 | async-start | bytes 9437184 | tf_op jit(solution)/shard_map/all_gather | solution.py:11
  10.0 639.7 %reduce-scatter.2.cloned.1.call-start = ((), (), s32[]{:S(2)}) async-start(), calls=%async_computation.2 | async-start | bytes 17825792 | tf_op jit(solution)/shard_map/reduce_scatter | solution.py:45
  504.5 147.6 %copy-start.1 = (bf16[256,256]{1,0:T(8,128)(2,1)S(1)}, bf16[256,256]{1,0:T(8,128)(2,1)}, u32[]{:S(2)}) copy-start(bf16[256,256]{1,0:T(8,128)(2,1)} %param.13) | copy-start | bytes 393220
  504.6 291.0 %all-reduce.2.cloned.1.call-start = ((), (), s32[]{:S(2)}) async-start(), calls=%async_computation.3 | async-start | bytes 524288 | tf_op jit(solution)/shard_map/psum | solution.py:54
Sparse Core Ops, SparseCore 0:
  10.3 95.1 all-gather.1
  504.7 144.9 reduce-scatter.1
  655.7 139.7 all-reduce.1
where the time goes:
time: 806 us; the launch traced here: 804 us
  waiting for transfers between devices  367 us (46%)
  matrix products  304 us (38%)
  local copies, waits for them, and re-layouts  87.5 us (11%)
  other arithmetic  30.8 us (4%)
  between operations  13.8 us (2%)
    dot_general x10, matrix products, add_group(): jnp.dot(both_place, both_vals, preferred_element_type=jnp.float32)  234 us
    reduce_scatter x1, waiting for transfers between devices, body(): lax.psum_scatter(partial_value.astype(jnp.bfloat16), 'row', scatter_dimen...  145 us
    psum x1, waiting for transfers between devices, body(): grad_weight = lax.psum(weight_term, ('row', 'col'))  141 us
    all_gather x1, waiting for transfers between devices, body(): block = lax.all_gather(masked, 'col', axis=0, tiled=True)  80.9 us
    dot_general x10, matrix products, add_group(): jnp.dot(pick, row_flat, preferred_element_type=jnp.float32)  46.4 us
    while x20, local copies, waits for them, and re-layouts  30.6 us
    convert_element_type x1, local copies, waits for them, and re-layouts, body(): partial_value.astype(jnp.bfloat16)  25.6 us
    dot_general x10, matrix products, add_group(): jnp.einsum('kab,kaf->kbf', tile_blk, gathered, preferred_element_type=jnp...  19.4 us
  transfers between devices with their start and end apart: 3, of which 3 were waited for; matrix products, arithmetic and copies ran while one was open for 2% of the time, Pallas kernels for 0%

commit v1 on v0

--- a/solution.py
+++ b/solution.py
@@ -1,3 +1,4 @@
+import functools
 import math
 import jax
 import jax.numpy as jnp
@@ -5,10 +6,19 @@
 from jax.sharding import PartitionSpec as P
 
 
+def _build_ladders(block_in, at_axis):
+    return jnp.concatenate(
+        lax.all_to_all(jnp.stack([block_in] * lax.axis_size("col")), "col", 0, 0), axis=at_axis
+    )
+
+
+order_case = functools.partial(_build_ladders, at_axis=0)
+
+
 def body(grad_out, preact, features, weight, tiles, tile_rows, tile_cols, live_counts):
     width = grad_out.shape[1]
     masked = jnp.where(preact > 0, grad_out, jnp.zeros_like(grad_out))
-    block = lax.all_gather(masked, "col", axis=0, tiled=True)
+    block = order_case(masked)
     row_count = block.shape[0] // 128
     row_flat = block.reshape(row_count, 128 * width)
     slots = tiles.shape[2]

time: 806 us -> 848 us (1.052)
  waiting for transfers between devices: 367 us -> 399 us
    all_gather x1 -> x0, waiting for transfers between devices: 80.9 us -> none  [body(): block = lax.all_gather(masked, 'col', axis=0, tiled=True)]
    all_to_all x0 -> x1, waiting for transfers between devices: none -> 80.1 us  [_build_ladders(): lax.all_to_all(jnp.stack([block_in] * lax.axis_size('col')), 'col', 0, 0)]
    reduce_scatter x1, waiting for transfers between devices: 145 us -> 178 us  [body(): lax.psum_scatter(partial_value.astype(jnp.bfloat16), 'row', scatter_dimen...]
    another operation x0 -> x2, local copies, waits for them, and re-layouts: none -> 17.3 us  [the longest x1 13.5 us: body(): row_flat = block.reshape(row_count, 128 * width)]
    reshape x1 -> x0, local copies, waits for them, and re-layouts: 13.4 us -> none  [body(): row_flat = block.reshape(row_count, 128 * width)]
where the time goes in v1:
time: 848 us; the launch traced here: 846 us
  waiting for transfers between devices  399 us (47%)
  matrix products  305 us (36%)
  local copies, waits for them, and re-layouts  91.2 us (11%)
  other arithmetic  29.8 us (4%)
  between operations  14.1 us (2%)
    dot_general x10, matrix products, add_group(): jnp.dot(both_place, both_vals, preferred_element_type=jnp.float32)  234 us
    reduce_scatter x1, waiting for transfers between devices, body(): lax.psum_scatter(partial_value.astype(jnp.bfloat16), 'row', scatter_dimen...  178 us
    psum x1, waiting for transfers between devices, body(): grad_weight = lax.psum(weight_term, ('row', 'col'))  141 us
    all_to_all x1, waiting for transfers between devices, _build_ladders(): lax.all_to_all(jnp.stack([block_in] * lax.axis_size('col')), 'col', 0, 0)  80.1 us
    dot_general x10, matrix products, add_group(): jnp.dot(pick, row_flat, preferred_element_type=jnp.float32)  46.4 us
    while x20, local copies, waits for them, and re-layouts  30.6 us
    convert_element_type x1, local copies, waits for them, and re-layouts, body(): partial_value.astype(jnp.bfloat16)  25.6 us
    dot_general x10, matrix products, add_group(): jnp.einsum('kab,kaf->kbf', tile_blk, gathered, preferred_element_type=jnp...  19.4 us
  transfers between devices with their start and end apart: 3, of which 3 were waited for; matrix products, arithmetic and copies ran while one was open for 2% of the time, Pallas kernels for 0%

profile of v1, /device:TPU:1, one launch (start us, length us, event | category | flops | bytes accessed | tf_op | source)
XLA Modules:
  0.0 845.7 jit_solution(4987231107171652965)
XLA Ops:
  12.8 6.3 all-to-all-start
  19.2 14.4 %copy.12 = bf16[1,1,320,128,128]{3,4,2,1,0:T(8,128)(2,1)} copy(bf16[1,1,320,128,128]{4,3,2,1,0:T(8,128)(2,1)} %param.14) | data formatting | bytes 20971520 | tf_op args[4]
  33.6 80.1 %all-to-all-done = bf16[8,2048,256]{2,1,0:T(8,128)(2,1)} async-done(((bf16[8,2048,256]{2,1,0:T(8,128)(2,1)}), bf16[8,2048,256]{2,1,0:T(8,128)(2,1)}, u32[]{:S(2)}, u32[]{:S(2)}) %all-to-all-start) | async-done | bytes 8388640 | tf_op jit(solution)/shard_map/all_to_all | solution.py:11
  113.7 13.5 %reshape_reshape.3 = bf16[128,32768]{1,0:T(8,128)(2,1)} reshape(bf16[8,2048,256]{2,1,0:T(8,128)(2,1)} %all-to-all-done) | data formatting | bytes 16777216 | tf_op jit(solution)/shard_map/reshape;reshape | solution.py:23
  127.1 343.1 %while.14 = (s32[]{:T(128)}, f32[256,32768]{1,0:T(8,128)}, s32[320]{0:T(512)S(1)}, s32[]{:T(128)}, bf16[320,128,128]{1,2,0:T(8,128)(2,1)}, /*index=5*/s32[320]{0...) while((s32[]{:T(128)}, f32[256,32768]{1,0:T(8,128)}, ...), condition=%wide.region_1.2_spmd.clone, body=%wide.region_0.1_spmd.clone.sunk | while | flops 1634766848 | bytes 110117888 | solution.py:53
  128.0 4.6 convolution_convert_fusion.3
  138.1 12.4 %convolution_add_fusion.2 = f32[256,32768]{1,0:T(8,128)} fusion(bf16[64,32768]{1,0:T(8,128)(2,1)S(1)} %bitcast.29, f32[256,32768]{1,0:T(8,128)} %get-tuple-element.281, pred[]{:T(512)S(6)} %compare.3, pred[256,32]{0,1:T(32,128)(4,1)S(1)} %fusion.34), kind=kOutput, calls=%fused_computation.3.clone.1 | convolution fusion | flops 1090535424 | bytes 71311360 | tf_op jit(solution)/shard_map/while/body/eval_jaxpr/dot_general | solution.py:50
  161.4 24.6 %convolution_add_fusion.2 = f32[256,32768]{1,0:T(8,128)} fusion(bf16[64,32768]{1,0:T(8,128)(2,1)S(1)} %bitcast.29, f32[256,32768]{1,0:T(8,128)} %get-tuple-element.281, pred[]{:T(512)S(6)} %compare.3, pred[256,32]{0,1:T(32,128)(4,1)S(1)} %fusion.34), kind=kOutput, calls=%fused_computation.3.clone.1 | convolution fusion | flops 1090535424 | bytes 71311360 | tf_op jit(solution)/shard_map/while/body/eval_jaxpr/dot_general | solution.py:50
  186.9 4.6 convolution_convert_fusion.3
  197.0 24.6 %convolution_add_fusion.2 = f32[256,32768]{1,0:T(8,128)} fusion(bf16[64,32768]{1,0:T(8,128)(2,1)S(1)} %bitcast.29, f32[256,32768]{1,0:T(8,128)} %get-tuple-element.281, pred[]{:T(512)S(6)} %compare.3, pred[256,32]{0,1:T(32,128)(4,1)S(1)} %fusion.34), kind=kOutput, calls=%fused_computation.3.clone.1 | convolution fusion | flops 1090535424 | bytes 71311360 | tf_op jit(solution)/shard_map/while/body/eval_jaxpr/dot_general | solution.py:50
  232.5 24.6 %convolution_add_fusion.2 = f32[256,32768]{1,0:T(8,128)} fusion(bf16[64,32768]{1,0:T(8,128)(2,1)S(1)} %bitcast.29, f32[256,32768]{1,0:T(8,128)} %get-tuple-element.281, pred[]{:T(512)S(6)} %compare.3, pred[256,32]{0,1:T(32,128)(4,1)S(1)} %fusion.34), kind=kOutput, calls=%fused_computation.3.clone.1 | convolution fusion | flops 1090535424 | bytes 71311360 | tf_op jit(solution)/shard_map/while/body/eval_jaxpr/dot_general | solution.py:50
  268.0 24.6 %convolution_add_fusion.2 = f32[256,32768]{1,0:T(8,128)} fusion(bf16[64,32768]{1,0:T(8,128)(2,1)S(1)} %bitcast.29, f32[256,32768]{1,0:T(8,128)} %get-tuple-element.281, pred[]{:T(512)S(6)} %compare.3, pred[256,32]{0,1:T(32,128)(4,1)S(1)} %fusion.34), kind=kOutput, calls=%fused_computation.3.clone.1 | convolution fusion | flops 1090535424 | bytes 71311360 | tf_op jit(solution)/shard_map/while/body/eval_jaxpr/dot_general | solution.py:50
  293.5 4.6 convolution_convert_fusion.3
  303.5 24.6 %convolution_add_fusion.2 = f32[256,32768]{1,0:T(8,128)} fusion(bf16[64,32768]{1,0:T(8,128)(2,1)S(1)} %bitcast.29, f32[256,32768]{1,0:T(8,128)} %get-tuple-element.281, pred[]{:T(512)S(6)} %compare.3, pred[256,32]{0,1:T(32,128)(4,1)S(1)} %fusion.34), kind=kOutput, calls=%fused_computation.3.clone.1 | convolution fusion | flops 1090535424 | bytes 71311360 | tf_op jit(solution)/shard_map/while/body/eval_jaxpr/dot_general | solution.py:50
  329.0 4.6 convolution_convert_fusion.3
  339.1 24.6 %convolution_add_fusion.2 = f32[256,32768]{1,0:T(8,128)} fusion(bf16[64,32768]{1,0:T(8,128)(2,1)S(1)} %bitcast.29, f32[256,32768]{1,0:T(8,128)} %get-tuple-element.281, pred[]{:T(512)S(6)} %compare.3, pred[256,32]{0,1:T(32,128)(4,1)S(1)} %fusion.34), kind=kOutput, calls=%fused_computation.3.clone.1 | convolution fusion | flops 1090535424 | bytes 71311360 | tf_op jit(solution)/shard_map/while/body/eval_jaxpr/dot_general | solution.py:50
  374.6 24.6 %convolution_add_fusion.2 = f32[256,32768]{1,0:T(8,128)} fusion(bf16[64,32768]{1,0:T(8,128)(2,1)S(1)} %bitcast.29, f32[256,32768]{1,0:T(8,128)} %get-tuple-element.281, pred[]{:T(512)S(6)} %compare.3, pred[256,32]{0,1:T(32,128)(4,1)S(1)} %fusion.34), kind=kOutput, calls=%fused_computation.3.clone.1 | convolution fusion | flops 1090535424 | bytes 71311360 | tf_op jit(solution)/shard_map/while/body/eval_jaxpr/dot_general | solution.py:50
  400.1 4.6 convolution_convert_fusion.3
  410.1 24.6 %convolution_add_fusion.2 = f32[256,32768]{1,0:T(8,128)} fusion(bf16[64,32768]{1,0:T(8,128)(2,1)S(1)} %bitcast.29, f32[256,32768]{1,0:T(8,128)} %get-tuple-element.281, pred[]{:T(512)S(6)} %compare.3, pred[256,32]{0,1:T(32,128)(4,1)S(1)} %fusion.34), kind=kOutput, calls=%fused_computation.3.clone.1 | convolution fusion | flops 1090535424 | bytes 71311360 | tf_op jit(solution)/shard_map/while/body/eval_jaxpr/dot_general | solution.py:50
  445.6 24.6 %convolution_add_fusion.2 = f32[256,32768]{1,0:T(8,128)} fusion(bf16[64,32768]{1,0:T(8,128)(2,1)S(1)} %bitcast.29, f32[256,32768]{1,0:T(8,128)} %get-tuple-element.281, pred[]{:T(512)S(6)} %compare.3, pred[256,32]{0,1:T(32,128)(4,1)S(1)} %fusion.34), kind=kOutput, calls=%fused_computation.3.clone.1 | convolution fusion | flops 1090535424 | bytes 71311360 | tf_op jit(solution)/shard_map/while/body/eval_jaxpr/dot_general | solution.py:50
  470.2 17.1 %convert_element_type.45 = bf16[256,32768]{1,0:T(8,128)(2,1)} convert(f32[256,32768]{1,0:T(8,128)} %get-tuple-element.171) | non-fusion elementwise | flops 8388608 | bytes 50331648 | tf_op jit(solution)/shard_map/convert_element_type | solution.py:56
  487.4 25.6 %convert_element_type.46 = bf16[32768,256]{1,0:T(8,128)(2,1)} reshape(bf16[256,32768]{1,0:T(8,128)(2,1)} %convert_element_type.45) | data formatting | bytes 33554432 | tf_op jit(solution)/shard_map/convert_element_type | solution.py:56
  513.1 178.1 %reduce-scatter.2.cloned.1.call-done = bf16[2048,256]{1,0:T(8,128)(2,1)} async-done(((bf16[32768,256]{1,0:T(8,128)(2,1)}), bf16[2048,256]{1,0:T(8,128)(2,1)}) %reduce-scatter.2.cloned.1.call-update) | async-done | bytes 1048592 | tf_op jit(solution)/shard_map/reduce_scatter | solution.py:55
  696.3 140.7 %all-reduce.2.cloned.1.call-done = f32[256,256]{0,1:T(8,128)} async-done(((f32[256,256]{0,1:T(8,128)}), f32[256,256]{0,1:T(8,128)}) %all-reduce.2.cloned.1.call-update) | async-done | bytes 262160 | tf_op jit(solution)/shard_map/psum | solution.py:64
  (105 shorter events, 98.2 us)
Async XLA Ops:
  7.2 684.0 %copy-start = (bf16[2048,256]{1,0:T(8,128)(2,1)S(1)}, bf16[2048,256]{1,0:T(8,128)(2,1)}, u32[]{:S(2)}) copy-start(bf16[2048,256]{1,0:T(8,128)(2,1)} %param.12) | copy-start | bytes 3145732
  12.8 6.4 copy-start.2
  12.8 6.4 copy-start.3
  12.8 100.9 %all-to-all-start = ((bf16[8,2048,256]{2,1,0:T(8,128)(2,1)}), bf16[8,2048,256]{2,1,0:T(8,128)(2,1)}, u32[]{:S(2)}, u32[]{:S(2)}) async-start(bf16[8,2048,256]{2,1,0:T(8,128)(2,1)} %stack.2), calls=%async_computation | async-start | bytes 16777216 | tf_op jit(solution)/shard_map/all_to_all | solution.py:11
  19.1 672.1 %reduce-scatter.2.cloned.1.call-start = ((), (), s32[]{:S(2)}) async-start(), calls=%async_computation.2 | async-start | bytes 17825792 | tf_op jit(solution)/shard_map/reduce_scatter | solution.py:55
  513.0 180.6 %copy-start.1 = (bf16[256,256]{1,0:T(8,128)(2,1)S(1)}, bf16[256,256]{1,0:T(8,128)(2,1)}, u32[]{:S(2)}) copy-start(bf16[256,256]{1,0:T(8,128)(2,1)} %param.13) | copy-start | bytes 393220
  513.0 324.0 %all-reduce.2.cloned.1.call-start = ((), (), s32[]{:S(2)}) async-start(), calls=%async_computation.3 | async-start | bytes 524288 | tf_op jit(solution)/shard_map/psum | solution.py:64
Sparse Core Ops, SparseCore 0:
  513.1 178.0 reduce-scatter.1
  697.2 139.7 all-reduce.1
